TPU v7x, 32 devices: a whole 2x2x4 slice. The times are simulated.
32 devices in a mesh: gy: 4 (over x, core), gx: 8 (over z, y).
Axes of the slice: x: 2, y: 2, z: 4, core: 2. Of those that a mesh axis runs over, the one named last changes fastest.
Arguments:
- tokens: bfloat16 [32, 128, 384], P('gy', 'gx'), may hold values from -6 to 6
- w_qkv: bfloat16 [384, 1152], replicated, may hold values from -1 to 1
- w_out: bfloat16 [384, 384], replicated, may hold values from -0.3125 to 0.3125
- block_mask: int32 [4, 16], P('gy', 'gx'), may hold values from 0 to 1, as said below
- grad_out: bfloat16 [32, 128, 384], P('gy', 'gx'), may hold values from -6 to 6
Outputs:
- mixed: bfloat16 [32, 128, 384], P('gy', 'gx')
- d_tokens: bfloat16 [32, 128, 384], P('gy', 'gx')
Inputs may be any that keep to these rules, and one draw needn't show every extreme that they name: `block_mask`: 1 marks a tissue block, 0 background.
All inputs are finite; a program needn't handle non-finite values.
Results may differ from a plain program's by a relative error of at most 0.017.
Values may be sent and summed in bfloat16 or wider, within the bound.
No kernel may reach another device: no remote copies, remote signals or barrier semaphores. Data moves between devices by JAX's collectives and lax.ppermute only.
A program may use at most 64 MiB of HBM per device.

v0:
```python
import jax
import jax.numpy as jnp
from jax import lax
from jax.sharding import PartitionSpec as P

NH = 6
HEAD_SIZE = 64
KS = 7
TISSUE_BLOCK = 8
NEG_FILL = -1e30


def with_halo(x, sides, width):
    for axis, dim in sides:
        size, length = (lax.axis_size(axis), x.shape[dim])
        up = [(i, (i + 1) % size) for i in range(size - 1)]
        down = [(j, i) for i, j in up]
        last = lax.slice_in_dim(x, length - width, length, axis=dim)
        first = lax.slice_in_dim(x, 0, width, axis=dim)
        before = lax.ppermute(last, axis, up)
        after = lax.ppermute(first, axis, down)
        x = jnp.concatenate([before, x, after], axis=dim)
    return x


def from_behind(value, axis, steps):
    count = lax.axis_size(axis)
    first, last = (max(0, -steps), min(count, count - steps))
    return lax.ppermute(value, axis, [(source, source + steps) for source in range(first, last)])


def block_means(field):
    tile_rows, tile_cols, width = field.shape
    grouped = field.astype(jnp.float32).reshape(
        tile_rows // TISSUE_BLOCK, TISSUE_BLOCK, tile_cols // TISSUE_BLOCK, TISSUE_BLOCK, width
    )
    return (jnp.sum(grouped, axis=(1, 3)) / TISSUE_BLOCK).reshape(-1, width)


def spread_blocks(blocks, tile_rows, tile_cols):
    shaped = blocks.reshape(tile_rows // TISSUE_BLOCK, tile_cols // TISSUE_BLOCK, -1)
    return jnp.repeat(jnp.repeat(shaped, TISSUE_BLOCK, 0), TISSUE_BLOCK, 1).reshape(
        tile_rows * tile_cols, -1
    )


def moving_window(extended, row_start, col_start, tile_rows, tile_cols):
    starts = (row_start, col_start) + tuple((0 for _ in extended.shape[2:]))
    extent = (tile_rows, tile_cols) + tuple(extended.shape[2:])
    return lax.dynamic_slice(extended, starts, extent)


def local(tokens, w_qkv, w_out, block_mask, grad_out):
    tile_rows, tile_cols, width = tokens.shape
    reachable_cells = KS // 2
    position_total = KS * KS
    token_count = tile_rows * tile_cols
    score_scale = HEAD_SIZE ** (-0.5)
    flat_tokens = tokens.reshape(token_count, width)
    qkv = jnp.dot(flat_tokens, w_qkv, preferred_element_type=jnp.float32).astype(jnp.bfloat16)
    query = qkv[:, :width].reshape(tile_rows, tile_cols, width)
    keys = qkv[:, width : 2 * width].reshape(tile_rows, tile_cols, width)
    values = qkv[:, 2 * width :].reshape(tile_rows, tile_cols, width)
    token_flag = spread_blocks(block_mask.astype(jnp.float32), tile_rows, tile_cols)
    row_place = (
        lax.axis_index("gy") * tile_rows
        + jnp.arange(tile_rows + 2 * reachable_cells)
        - reachable_cells
    )
    col_place = (
        lax.axis_index("gx") * tile_cols
        + jnp.arange(tile_cols + 2 * reachable_cells)
        - reachable_cells
    )
    row_inside = (row_place >= 0) & (row_place < tile_rows * lax.axis_size("gy"))
    col_inside = (col_place >= 0) & (col_place < tile_cols * lax.axis_size("gx"))
    inside = row_inside[:, None] & col_inside[None, :]

    def window(extended, position):
        return moving_window(extended, position // KS, position % KS, tile_rows, tile_cols)

    pooled_keys = block_means(keys).astype(jnp.bfloat16)
    pooled_vals = block_means(values).astype(jnp.bfloat16)
    pool_flag = block_mask.reshape(-1).astype(jnp.bfloat16)
    kv_ext = with_halo(
        jnp.concatenate([keys, values], axis=2), (("gy", 0), ("gx", 1)), reachable_cells
    )
    row_keys, row_vals, row_flag = (
        lax.all_gather(pooled_keys, "gx", axis=0, tiled=True),
        lax.all_gather(pooled_vals, "gx", axis=0, tiled=True),
        lax.all_gather(pool_flag, "gx", axis=0, tiled=True),
    )
    col_keys, col_vals, col_flag = (
        lax.all_gather(pooled_keys, "gy", axis=0, tiled=True),
        lax.all_gather(pooled_vals, "gy", axis=0, tiled=True),
        lax.all_gather(pool_flag, "gy", axis=0, tiled=True),
    )
    query_heads = query.reshape(token_count, NH, HEAD_SIZE)

    def score_step(position, collected):
        key_win = window(kv_ext, position)[:, :, :width].reshape(token_count, NH, HEAD_SIZE)
        scores = (
            jnp.einsum("tnd,tnd->nt", query_heads, key_win, preferred_element_type=jnp.float32)
            * score_scale
        )
        valid = window(inside, position).reshape(token_count)
        masked = jnp.where(valid[None, :], scores, NEG_FILL)
        return lax.dynamic_update_index_in_dim(collected, masked, position, 0)

    local_s = lax.fori_loop(
        0, position_total, score_step, jnp.zeros((position_total, NH, token_count), jnp.float32)
    )

    def pool_scores(pool_keys, flags):
        scores = (
            jnp.einsum(
                "tnd,pnd->ntp",
                query_heads,
                pool_keys.reshape(-1, NH, HEAD_SIZE),
                preferred_element_type=jnp.float32,
            )
            * score_scale
        )
        return jnp.where(flags[None, None, :] > 0, scores, NEG_FILL)

    row_s = pool_scores(row_keys, row_flag)
    col_s = pool_scores(col_keys, col_flag)
    top = jnp.maximum(jnp.maximum(jnp.max(local_s, 0), jnp.max(row_s, -1)), jnp.max(col_s, -1))
    total = (
        jnp.sum(jnp.exp(local_s - top), 0)
        + jnp.sum(jnp.exp(row_s - top[:, :, None]), -1)
        + jnp.sum(jnp.exp(col_s - top[:, :, None]), -1)
    )
    lse = top + jnp.log(total)
    local_probs = jnp.exp(local_s - lse)
    row_pf = jnp.exp(row_s - lse[:, :, None])
    col_pf = jnp.exp(col_s - lse[:, :, None])
    row_ph = row_pf.astype(jnp.bfloat16)
    col_ph = col_pf.astype(jnp.bfloat16)

    def value_step(position, output):
        value_win = window(kv_ext, position)[:, :, width:].reshape(token_count, NH, HEAD_SIZE)
        probs = lax.dynamic_index_in_dim(local_probs, position, 0, keepdims=False)
        return output + probs.T[:, :, None] * value_win

    output = lax.fori_loop(
        0, position_total, value_step, jnp.zeros((token_count, NH, HEAD_SIZE), jnp.float32)
    )
    output = output + jnp.einsum(
        "ntp,pnd->tnd",
        row_ph,
        row_vals.reshape(-1, NH, HEAD_SIZE),
        preferred_element_type=jnp.float32,
    )
    output = output + jnp.einsum(
        "ntp,pnd->tnd",
        col_ph,
        col_vals.reshape(-1, NH, HEAD_SIZE),
        preferred_element_type=jnp.float32,
    )
    attended = output.reshape(token_count, width).astype(jnp.bfloat16)
    gated = attended * token_flag.astype(jnp.bfloat16)
    mixed = (
        flat_tokens.astype(jnp.float32) + jnp.dot(gated, w_out, preferred_element_type=jnp.float32)
    ).astype(jnp.bfloat16)
    grad_flat = grad_out.reshape(token_count, width)
    d_att = (
        jnp.einsum("tc,ec->te", grad_flat, w_out, preferred_element_type=jnp.float32) * token_flag
    ).astype(jnp.bfloat16)
    datt_heads = d_att.reshape(token_count, NH, HEAD_SIZE)
    delta = jnp.einsum(
        "tnd,tnd->nt",
        datt_heads,
        attended.reshape(token_count, NH, HEAD_SIZE),
        preferred_element_type=jnp.float32,
    )

    def pool_backward(prob_full, prob_half, pool_keys, pool_vals):
        key_heads = pool_keys.reshape(-1, NH, HEAD_SIZE)
        value_heads = pool_vals.reshape(-1, NH, HEAD_SIZE)
        prob_grad = jnp.einsum(
            "tnd,pnd->ntp", datt_heads, value_heads, preferred_element_type=jnp.float32
        )
        score_grad = (prob_full * (prob_grad - delta[:, :, None])).astype(jnp.bfloat16)
        query_part = (
            jnp.einsum("ntp,pnd->tnd", score_grad, key_heads, preferred_element_type=jnp.float32)
            * score_scale
        )
        key_part = (
            jnp.einsum("ntp,tnd->pnd", score_grad, query_heads, preferred_element_type=jnp.float32)
            * score_scale
        )
        value_part = jnp.einsum(
            "ntp,tnd->pnd", prob_half, datt_heads, preferred_element_type=jnp.float32
        )
        return (query_part, key_part.reshape(-1, width), value_part.reshape(-1, width))

    row_dq, row_dk, row_dv = pool_backward(row_pf, row_ph, row_keys, row_vals)
    col_dq, col_dk, col_dv = pool_backward(col_pf, col_ph, col_keys, col_vals)
    block_count = pooled_keys.shape[0]
    whole_row_dk, whole_row_dv = (
        lax.psum(row_dk.astype(jnp.bfloat16), "gx").astype(jnp.float32),
        lax.psum(row_dv.astype(jnp.bfloat16), "gx").astype(jnp.float32),
    )
    whole_col_dk, whole_col_dv = (
        lax.psum(col_dk.astype(jnp.bfloat16), "gy").astype(jnp.float32),
        lax.psum(col_dv.astype(jnp.bfloat16), "gy").astype(jnp.float32),
    )
    row_start = lax.axis_index("gx") * block_count
    col_start = lax.axis_index("gy") * block_count
    own_row_dk = lax.dynamic_slice_in_dim(whole_row_dk, row_start, block_count, 0)
    own_row_dv = lax.dynamic_slice_in_dim(whole_row_dv, row_start, block_count, 0)
    own_col_dk = lax.dynamic_slice_in_dim(whole_col_dk, col_start, block_count, 0)
    own_col_dv = lax.dynamic_slice_in_dim(whole_col_dv, col_start, block_count, 0)

    def query_step(position, grad_query):
        both_win = window(kv_ext, position)
        key_win = both_win[:, :, :width].reshape(token_count, NH, HEAD_SIZE)
        value_win = both_win[:, :, width:].reshape(token_count, NH, HEAD_SIZE)
        prob_grad = jnp.einsum(
            "tnd,tnd->nt", datt_heads, value_win, preferred_element_type=jnp.float32
        )
        probs = lax.dynamic_index_in_dim(local_probs, position, 0, keepdims=False)
        score_grad = probs * (prob_grad - delta)
        return grad_query + (score_grad.T[:, :, None] * key_win * score_scale).reshape(
            token_count, width
        )

    grad_query = lax.fori_loop(
        0, position_total, query_step, (row_dq + col_dq).reshape(token_count, width)
    )

    def return_step(position, ext_grad):
        both_win = window(kv_ext, position)
        value_win = both_win[:, :, width:].reshape(token_count, NH, HEAD_SIZE)
        prob_grad = jnp.einsum(
            "tnd,tnd->nt", datt_heads, value_win, preferred_element_type=jnp.float32
        )
        probs = lax.dynamic_index_in_dim(local_probs, position, 0, keepdims=False)
        score_grad = probs * (prob_grad - delta)
        key_term = (score_grad.T[:, :, None] * query_heads * score_scale).reshape(
            tile_rows, tile_cols, width
        )
        value_term = (probs.T[:, :, None] * datt_heads).reshape(tile_rows, tile_cols, width)
        updated = window(ext_grad, position) + jnp.concatenate([key_term, value_term], axis=2)
        return lax.dynamic_update_slice(ext_grad, updated, (position // KS, position % KS, 0))

    ext_grad = lax.fori_loop(
        0,
        position_total,
        return_step,
        jnp.zeros(
            (tile_rows + 2 * reachable_cells, tile_cols + 2 * reachable_cells, 2 * width),
            jnp.float32,
        ),
    )
    col_moves = (
        (-1, slice(0, reachable_cells), slice(tile_cols, tile_cols + reachable_cells)),
        (
            1,
            slice(tile_cols + reachable_cells, tile_cols + 2 * reachable_cells),
            slice(reachable_cells, 2 * reachable_cells),
        ),
    )
    for step_by, source_span, target_span in col_moves:
        arrived = from_behind(ext_grad[:, source_span].astype(jnp.bfloat16), "gx", step_by).astype(
            jnp.float32
        )
        ext_grad = ext_grad.at[:, target_span].add(arrived)
    ext_grad = ext_grad[:, reachable_cells : reachable_cells + tile_cols]
    row_moves = (
        (-1, slice(0, reachable_cells), slice(tile_rows, tile_rows + reachable_cells)),
        (
            1,
            slice(tile_rows + reachable_cells, tile_rows + 2 * reachable_cells),
            slice(reachable_cells, 2 * reachable_cells),
        ),
    )
    for step_by, source_span, target_span in row_moves:
        arrived = from_behind(ext_grad[source_span].astype(jnp.bfloat16), "gy", step_by).astype(
            jnp.float32
        )
        ext_grad = ext_grad.at[target_span].add(arrived)
    own_grad = ext_grad[reachable_cells : reachable_cells + tile_rows].reshape(
        token_count, 2 * width
    )
    grad_keys = own_grad[:, :width]
    grad_vals = own_grad[:, width:]
    grad_keys = grad_keys + spread_blocks(
        (own_row_dk + own_col_dk) / TISSUE_BLOCK, tile_rows, tile_cols
    )
    grad_vals = grad_vals + spread_blocks(
        (own_row_dv + own_col_dv) / TISSUE_BLOCK, tile_rows, tile_cols
    )
    d_qkv = jnp.concatenate([grad_query, grad_keys, grad_vals], axis=1).astype(jnp.bfloat16)
    d_tokens = (
        grad_flat.astype(jnp.float32)
        + jnp.einsum("tf,cf->tc", d_qkv, w_qkv, preferred_element_type=jnp.float32)
    ).astype(jnp.bfloat16)
    return (
        mixed.reshape(tile_rows, tile_cols, width),
        d_tokens.reshape(tile_rows, tile_cols, width),
    )


def solution(mesh):
    placed = (P("gy", "gx", None), P(), P(), P("gy", "gx"), P("gy", "gx", None))
    return jax.shard_map(
        local,
        mesh=mesh,
        in_specs=placed,
        out_specs=(P("gy", "gx", None), P("gy", "gx", None)),
        check_vma=False,
    )
```

profile of v0, /device:TPU:1, one launch (start us, length us, event | category | flops | bytes accessed | tf_op | source)
XLA Modules:
  0.0 717.1 jit_solution(2901687024737776675)
XLA Ops:
  3.1 4.5 collective-permute-start
  9.6 21.7 %all-gather.2 = bf16[8,2,384]{2,1,0:T(2,128)(2,1)S(1)} all-gather(bf16[1,2,384]{2,1,0:T(2,128)(2,1)S(1)} %fusion.49), channel_id=1, replica_groups=mesh['gy'=4,'gx'=8] {'gx'}, dimensions={0}, use_global_device_ids=true | all-gather | bytes 13824 | tf_op jit(solution)/shard_map/all_gather | solution.py:89
  31.3 9.7 %all-gather.3 = bf16[4,2,384]{2,1,0:T(2,128)(2,1)S(1)} all-gather(bf16[1,2,384]{2,1,0:T(2,128)(2,1)S(1)} %fusion.49), channel_id=1, replica_groups=mesh['gy'=4,'gx'=8] {'gy'}, dimensions={0}, use_global_device_ids=true | all-gather | bytes 7680 | tf_op jit(solution)/shard_map/all_gather | solution.py:94
  44.1 16.2 %all-reduce = bf16[16]{0:T(256)(128)(2,1)S(1)} all-reduce(bf16[16]{0:T(256)(128)(2,1)S(1)} %dynamic-update-slice.12), channel_id=2, replica_groups=mesh['gy'=4,'gx'=8] {'gx'}, use_global_device_ids=true, to_apply=%add | all-reduce | flops 16 | bytes 64
  62.5 9.3 %all-reduce.1 = bf16[8]{0:T(256)(128)(2,1)S(1)} all-reduce(bf16[8]{0:T(256)(128)(2,1)S(1)} %dynamic-update-slice.13), channel_id=3, replica_groups=mesh['gy'=4,'gx'=8] {'gy'}, use_global_device_ids=true, to_apply=%add.1 | all-reduce | flops 8 | bytes 32
  77.0 21.3 %all-gather.4 = bf16[8,2,384]{2,1,0:T(2,128)(2,1)S(1)} all-gather(bf16[1,2,384]{2,1,0:T(2,128)(2,1)S(1)} %fusion.50), channel_id=1, replica_groups=mesh['gy'=4,'gx'=8] {'gx'}, dimensions={0}, use_global_device_ids=true | all-gather | bytes 13824 | tf_op jit(solution)/shard_map/all_gather | solution.py:90
  98.4 9.9 %all-gather.5 = bf16[4,2,384]{2,1,0:T(2,128)(2,1)S(1)} all-gather(bf16[1,2,384]{2,1,0:T(2,128)(2,1)S(1)} %fusion.50), channel_id=1, replica_groups=mesh['gy'=4,'gx'=8] {'gy'}, dimensions={0}, use_global_device_ids=true | all-gather | bytes 7680 | tf_op jit(solution)/shard_map/all_gather | solution.py:95
  110.5 37.0 %while.65 = (s32[]{:T(128)}, f32[49,6,128]{2,1,0:T(8,128)S(1)}, pred[14,22]{1,0:T(8,128)(4,1)S(1)}, bf16[14,22,768]{2,1,0:T(8,128)(2,1)S(1)}, bf16[128,6,64]{2,1...) while((s32[]{:T(128)}, f32[49,6,128]{2,1,0:T(8,128)S(1)}, ...), condition=%wide.region_1.0_spmd, body=%wide.region_0.0_spmd.sunk | while | flops 197396 | bytes 608564 | solution.py:110
  150.2 4.1 exp.21
  154.3 68.9 %while.68 = (s32[]{:T(128)}, f32[128,6,64]{2,1,0:T(8,128)S(1)}, f32[49,6,128]{1,2,0:T(8,128)}, bf16[14,22,768]{2,1,0:T(8,128)(2,1)S(1)}, s32[]{:T(128)}, /*index...) while((s32[]{:T(128)}, f32[128,6,64]{2,1,0:T(8,128)S(1)}, ...), condition=%wide.region_10.11_spmd.clone, body=%wide.region_9.10_spmd.clone.sunk | while | flops 196630 | bytes 1287498 | solution.py:146
  228.7 43.8 %while.66 = (s32[]{:T(128)}, f32[128,384]{0,1:T(8,128)S(1)}, f32[49,6,128]{2,1,0:T(8,128)S(1)}, bf16[14,22,768]{2,1,0:T(8,128)(2,1)S(1)}, bf16[128,6,64]{2,1,0:T...) while((s32[]{:T(128)}, f32[128,384]{0,1:T(8,128)S(1)}, ...), condition=%wide.region_13.14_spmd, body=%wide.region_12.13_spmd.sunk | while | flops 394005 | bytes 2089296 | solution.py:229
  273.5 362.1 %while.67 = (s32[]{:T(128)}, f32[14,22,768]{2,1,0:T(8,128)}, f32[49,6,128]{1,2,0:T(8,128)}, bf16[14,22,768]{2,1,0:T(8,128)(2,1)S(1)}, bf16[128,6,64]{2,1,0:T(8,1...) while((s32[]{:T(128)}, f32[14,22,768]{2,1,0:T(8,128)}, ...), condition=%wide.region_15.16_spmd, body=%wide.region_14.15_spmd.sunk | while | flops 639765 | bytes 3960160 | solution.py:248
  277.5 3.5 dynamic_update_slice.25
  284.9 3.5 dynamic_update_slice.25
  292.3 3.5 dynamic_update_slice.25
  299.8 3.5 dynamic_update_slice.25
  307.2 3.5 dynamic_update_slice.25
  314.6 3.5 dynamic_update_slice.25
  322.1 3.5 dynamic_update_slice.25
  329.5 3.5 dynamic_update_slice.25
  336.9 3.5 dynamic_update_slice.25
  344.4 3.5 dynamic_update_slice.25
  351.8 3.5 dynamic_update_slice.25
  359.2 3.5 dynamic_update_slice.25
  366.7 3.5 dynamic_update_slice.25
  374.1 3.5 dynamic_update_slice.25
  381.5 3.5 dynamic_update_slice.25
  389.0 3.5 dynamic_update_slice.25
  396.4 3.5 dynamic_update_slice.25
  403.8 3.5 dynamic_update_slice.25
  411.3 3.5 dynamic_update_slice.25
  418.7 3.5 dynamic_update_slice.25
  426.1 3.5 dynamic_update_slice.25
  433.5 3.5 dynamic_update_slice.25
  441.0 3.5 dynamic_update_slice.25
  448.4 3.5 dynamic_update_slice.25
  455.8 3.5 dynamic_update_slice.25
  463.3 3.5 dynamic_update_slice.25
  470.7 3.5 dynamic_update_slice.25
  478.1 3.5 dynamic_update_slice.25
  485.6 3.4 dynamic_update_slice.25
  492.9 3.4 dynamic_update_slice.25
  500.3 3.4 dynamic_update_slice.25
  507.7 3.4 dynamic_update_slice.25
  515.1 3.4 dynamic_update_slice.25
  522.5 3.4 dynamic_update_slice.25
  529.9 3.4 dynamic_update_slice.25
  537.3 3.4 dynamic_update_slice.25
  544.7 3.4 dynamic_update_slice.25
  552.0 3.4 dynamic_update_slice.25
  559.4 3.4 dynamic_update_slice.25
  566.7 3.4 dynamic_update_slice.25
  574.1 3.4 dynamic_update_slice.25
  581.4 3.4 dynamic_update_slice.25
  588.8 3.3 dynamic_update_slice.25
  596.1 3.3 dynamic_update_slice.25
  603.3 3.3 dynamic_update_slice.25
  610.6 3.3 dynamic_update_slice.25
  647.5 3.4 collective-permute-start.5
  653.5 3.5 scatter-add.15
  657.9 3.8 collective-permute-start.6
  663.3 28.1 %all-reduce.2 = (bf16[16,384]{1,0:T(8,128)(2,1)S(1)}, bf16[16,384]{1,0:T(8,128)(2,1)S(1)}) all-reduce(bf16[16,384]{1,0:T(8,128)(2,1)S(1)} %convert_element_type.237, bf16[16,384]{1,0:T(8,128)(2,1)S(1)} %convert_element_type.229), channel_id=1, replica_groups=mesh['gy'=4,'gx'=8] {'gx'}, use_global_device_ids=true, to_apply=%region_18.19 | all-reduce | flops 12288 | bytes 49152 | tf_op jit(solution)/shard_map/psum | solution.py:203
  691.5 16.6 %all-reduce.3 = (bf16[8,384]{1,0:T(8,128)(2,1)S(1)}, bf16[8,384]{1,0:T(8,128)(2,1)S(1)}) all-reduce(bf16[8,384]{1,0:T(8,128)(2,1)S(1)} %convert_element_type.241, bf16[8,384]{1,0:T(8,128)(2,1)S(1)} %convert_element_type.233), channel_id=1, replica_groups=mesh['gy'=4,'gx'=8] {'gy'}, use_global_device_ids=true, to_apply=%region_19.20 | all-reduce | flops 6144 | bytes 24576 | tf_op jit(solution)/shard_map/psum | solution.py:207
  710.3 4.2 collective-permute-start.7
  (1489 shorter events, 386.6 us)
Async XLA Ops:
  0.6 1.2 copy-start
  0.6 71.7 %copy-start.2 = (bf16[384,384]{1,0:T(8,128)(2,1)S(1)}, bf16[384,384]{1,0:T(8,128)(2,1)}, u32[]{:S(2)}) copy-start(bf16[384,384]{1,0:T(8,128)(2,1)} %param.23) | copy-start | bytes 884740
  3.1 70.4 %collective-permute-start = (bf16[3,16,768]{2,1,0:T(8,128)(2,1)S(1)}, bf16[3,16,768]{2,1,0:T(8,128)(2,1)S(1)}, u32[]{:S(2)}, u32[]{:S(2)}) collective-permute-start(bf16[3,16,768]{2,1,0:T(8,128)(2,1)S(1)} %get-tuple-element.772), channel_id=1, source_target_pairs={{0,8},{8,16},{16,24},{1,9},{9,17},{17,25},{2,10},{10,18},{18,26},{... | collective-permute-start | bytes 221192 | tf_op jit(solution)/shard_map/ppermute | solution.py:20
  7.6 65.9 %collective-permute-start.1 = (bf16[3,16,768]{2,1,0:T(8,128)(2,1)S(1)}, bf16[3,16,768]{2,1,0:T(8,128)(2,1)S(1)}, u32[]{:S(2)}, u32[]{:S(2)}) collective-permute-start(bf16[3,16,768]{2,1,0:T(8,128)(2,1)S(1)} %get-tuple-element.773), channel_id=1, source_target_pairs={{8,0},{16,8},{24,16},{9,1},{17,9},{25,17},{10,2},{18,10},{26,18},{... | collective-permute-start | bytes 221192 | tf_op jit(solution)/shard_map/ppermute | solution.py:21
  41.0 67.2 %copy-start.1 = (bf16[128,384]{0,1:T(8,128)(2,1)}, bf16[128,384]{0,1:T(8,128)(2,1)S(1)}, u32[]{:S(2)}) copy-start(bf16[128,384]{0,1:T(8,128)(2,1)S(1)} %copy.82) | copy-start | bytes 294916
  73.6 35.1 %collective-permute-start.2 = (bf16[14,3,768]{2,1,0:T(4,128)(2,1)S(1)}, bf16[14,3,768]{2,1,0:T(4,128)(2,1)S(1)}, u32[]{:S(2)}, u32[]{:S(2)}) collective-permute-start(bf16[14,3,768]{2,1,0:T(4,128)(2,1)S(1)} %get-tuple-element.767), channel_id=1, source_target_pairs={{0,1},{1,2},{2,3},{3,4},{4,5},{5,6},{6,7},{8,9},{9,10},{10,11},{11... | collective-permute-start | bytes 193544 | tf_op jit(solution)/shard_map/ppermute | solution.py:20
  74.9 34.5 %collective-permute-start.3 = (bf16[14,3,768]{2,1,0:T(4,128)(2,1)S(1)}, bf16[14,3,768]{2,1,0:T(4,128)(2,1)}, u32[]{:S(2)}, u32[]{:S(2)}) collective-permute-start(bf16[14,3,768]{2,1,0:T(4,128)(2,1)S(1)} %get-tuple-element.768), channel_id=1, source_target_pairs={{1,0},{2,1},{3,2},{4,3},{5,4},{6,5},{7,6},{9,8},{10,9},{11,10},{12... | collective-permute-start | bytes 193544 | tf_op jit(solution)/shard_map/ppermute | solution.py:21
  108.7 0.6 copy-start.8
  147.7 79.6 %copy-start.3 = (f32[6,128]{1,0:T(8,128)}, f32[6,128]{1,0:T(8,128)S(1)}, u32[]{:S(2)}) copy-start(f32[6,128]{1,0:T(8,128)S(1)} %log_add_fusion) | copy-start | bytes 9220
  224.6 4.1 copy-start.4
  224.8 4.0 copy-start.5
  635.7 27.3 %copy-start.7 = (bf16[16,6,64]{2,0,1:T(8,128)(2,1)S(1)}, bf16[16,6,64]{2,0,1:T(8,128)(2,1)}, u32[]{:S(2)}) copy-start(bf16[16,6,64]{2,0,1:T(8,128)(2,1)} %fusion.18) | copy-start | bytes 36868
  636.7 5.8 collective-permute-start.4
  641.8 74.2 %copy-start.6 = (bf16[8,16,384]{2,1,0:T(8,128)(2,1)S(1)}, bf16[8,16,384]{2,1,0:T(8,128)(2,1)}, u32[]{:S(2)}) copy-start(bf16[8,16,384]{2,1,0:T(8,128)(2,1)} %param.25) | copy-start | bytes 294916
  647.5 5.0 collective-permute-start.5
  657.9 51.4 %collective-permute-start.6 = (bf16[3,16,768]{2,1,0:T(8,128)(2,1)S(1)}, bf16[3,16,768]{2,1,0:T(8,128)(2,1)S(1)}, u32[]{:S(2)}, u32[]{:S(2)}) collective-permute-start(bf16[3,16,768]{2,1,0:T(8,128)(2,1)S(1)} %slice.252), channel_id=1, source_target_pairs={{8,0},{16,8},{24,16},{9,1},{17,9},{25,17},{10,2},{18,10},{26,18},{... | collective-permute-start | bytes 221192 | tf_op jit(solution)/shard_map/ppermute | solution.py:29
  710.3 5.6 collective-permute-start.7
where the time goes:
time: 731 us; the launch traced here: 717 us
  local copies, waits for them, and re-layouts  356 us (49%)
  other arithmetic  177 us (24%)
  blocking collectives  133 us (18%)
  starting transfers between devices  21.7 us (3%)
  loops' own time  13.3 us (2%)
  matrix products  11.1 us (2%)
    dynamic_update_slice x49, local copies, waits for them, and re-layouts, return_step(): lax.dynamic_update_slice(ext_grad, updated, (position // KS, position % K...  169 us
    add x49, other arithmetic, return_step(): window(ext_grad, position) + jnp.concatenate([key_term, value_term], axis=2)  55.9 us
    transpose x49, other arithmetic, return_step(): score_grad.T[:, :, None] * query_heads * score_scale  42.1 us
    transpose x49, local copies, waits for them, and re-layouts, return_step(): probs.T[:, :, None] * datt_heads  41.7 us
    transpose x49, local copies, waits for them, and re-layouts, value_step(): return output + probs.T[:, :, None] * value_win  41.7 us
    psum x1, blocking collectives, local(): lax.psum(row_dv.astype(jnp.bfloat16), 'gx').astype(jnp.float32)  28.1 us
    unnamed x2, blocking collectives  25.5 us
    all_gather x1, blocking collectives, local(): lax.all_gather(pooled_keys, 'gx', axis=0, tiled=True)  21.7 us
  transfers between devices with their start and end apart: 8, of which 3 were waited for; matrix products, arithmetic and copies ran while one was open for 2% of the time, Pallas kernels for 0%

commit v1 on v0

--- a/solution.py
+++ b/solution.py
@@ -1,13 +1,23 @@
+import functools
 import jax
 import jax.numpy as jnp
 from jax import lax
 from jax.sharding import PartitionSpec as P
+from jax.lax import all_gather
 
 NH = 6
 HEAD_SIZE = 64
 KS = 7
 TISSUE_BLOCK = 8
 NEG_FILL = -1e30
+
+
+def detail_slot(raw, dev_axis):
+    outcome_arr = all_gather(raw, dev_axis).sum(axis=0)
+    return outcome_arr
+
+
+turn_rings = functools.partial(detail_slot, dev_axis="gx")
 
 
 def with_halo(x, sides, width):
@@ -200,7 +210,7 @@
     block_count = pooled_keys.shape[0]
     whole_row_dk, whole_row_dv = (
         lax.psum(row_dk.astype(jnp.bfloat16), "gx").astype(jnp.float32),
-        lax.psum(row_dv.astype(jnp.bfloat16), "gx").astype(jnp.float32),
+        turn_rings(row_dv.astype(jnp.bfloat16)).astype(jnp.float32),
     )
     whole_col_dk, whole_col_dv = (
         lax.psum(col_dk.astype(jnp.bfloat16), "gy").astype(jnp.float32),

time: 731 us -> 797 us (1.090)
  local copies, waits for them, and re-layouts: 356 us -> 391 us
  blocking collectives: 133 us -> 163 us
    dynamic_slice x49, local copies, waits for them, and re-layouts: 4.44 us -> 37.7 us  [moving_window(): return lax.dynamic_slice(extended, starts, extent)]
    all_gather x0 -> x1, blocking collectives: none -> 24.5 us  [detail_slot(): outcome_arr = all_gather(raw, dev_axis).sum(axis=0)]
where the time goes in v1:
time: 797 us; the launch traced here: 782 us
  local copies, waits for them, and re-layouts  391 us (49%)
  other arithmetic  177 us (22%)
  blocking collectives  163 us (20%)
  starting transfers between devices  18.3 us (2%)
  loops' own time  12.8 us (2%)
  matrix products  12 us (2%)
    dynamic_update_slice x49, local copies, waits for them, and re-layouts, return_step(): lax.dynamic_update_slice(ext_grad, updated, (position // KS, position % K...  169 us
    add x49, other arithmetic, return_step(): window(ext_grad, position) + jnp.concatenate([key_term, value_term], axis=2)  55.9 us
    transpose x49, other arithmetic, return_step(): score_grad.T[:, :, None] * query_heads * score_scale  42.1 us
    transpose x49, local copies, waits for them, and re-layouts, return_step(): probs.T[:, :, None] * datt_heads  41.7 us
    transpose x49, local copies, waits for them, and re-layouts, value_step(): return output + probs.T[:, :, None] * value_win  41.7 us
    dynamic_slice x49, local copies, waits for them, and re-layouts, moving_window(): return lax.dynamic_slice(extended, starts, extent)  37.7 us
    psum x1, blocking collectives, local(): lax.psum(row_dk.astype(jnp.bfloat16), 'gx').astype(jnp.float32)  26.8 us
    unnamed x2, blocking collectives  25.5 us
  transfers between devices with their start and end apart: 8, of which 3 were waited for; matrix products, arithmetic and copies ran while one was open for 2% of the time, Pallas kernels for 0%

profile of v1, /device:TPU:1, one launch (start us, length us, event | category | flops | bytes accessed | tf_op | source)
XLA Modules:
  0.0 781.6 jit_solution(6960298157025809199)
XLA Ops:
  3.1 4.5 collective-permute-start
  9.6 21.7 %all-gather.2 = bf16[8,2,384]{2,1,0:T(2,128)(2,1)S(1)} all-gather(bf16[1,2,384]{2,1,0:T(2,128)(2,1)S(1)} %fusion.49), channel_id=1, replica_groups=mesh['gy'=4,'gx'=8] {'gx'}, dimensions={0}, use_global_device_ids=true | all-gather | bytes 13824 | tf_op jit(solution)/shard_map/all_gather | solution.py:99
  31.3 9.7 %all-gather.3 = bf16[4,2,384]{2,1,0:T(2,128)(2,1)S(1)} all-gather(bf16[1,2,384]{2,1,0:T(2,128)(2,1)S(1)} %fusion.49), channel_id=1, replica_groups=mesh['gy'=4,'gx'=8] {'gy'}, dimensions={0}, use_global_device_ids=true | all-gather | bytes 7680 | tf_op jit(solution)/shard_map/all_gather | solution.py:104
  44.1 16.2 %all-reduce = bf16[16]{0:T(256)(128)(2,1)S(1)} all-reduce(bf16[16]{0:T(256)(128)(2,1)S(1)} %dynamic-update-slice.12), channel_id=2, replica_groups=mesh['gy'=4,'gx'=8] {'gx'}, use_global_device_ids=true, to_apply=%add | all-reduce | flops 16 | bytes 64
  62.5 9.3 %all-reduce.1 = bf16[8]{0:T(256)(128)(2,1)S(1)} all-reduce(bf16[8]{0:T(256)(128)(2,1)S(1)} %dynamic-update-slice.13), channel_id=3, replica_groups=mesh['gy'=4,'gx'=8] {'gy'}, use_global_device_ids=true, to_apply=%add.1 | all-reduce | flops 8 | bytes 32
  78.7 21.3 %all-gather.4 = bf16[8,2,384]{2,1,0:T(2,128)(2,1)S(1)} all-gather(bf16[1,2,384]{2,1,0:T(2,128)(2,1)S(1)} %fusion.50), channel_id=1, replica_groups=mesh['gy'=4,'gx'=8] {'gx'}, dimensions={0}, use_global_device_ids=true | all-gather | bytes 13824 | tf_op jit(solution)/shard_map/all_gather | solution.py:100
  100.7 9.9 %all-gather.5 = bf16[4,2,384]{2,1,0:T(2,128)(2,1)S(1)} all-gather(bf16[1,2,384]{2,1,0:T(2,128)(2,1)S(1)} %fusion.50), channel_id=1, replica_groups=mesh['gy'=4,'gx'=8] {'gy'}, dimensions={0}, use_global_device_ids=true | all-gather | bytes 7680 | tf_op jit(solution)/shard_map/all_gather | solution.py:105
  112.2 69.8 %while.65 = (s32[]{:T(128)}, f32[49,6,128]{2,1,0:T(8,128)S(1)}, pred[14,22]{1,0:T(8,128)(4,1)}, bf16[14,22,768]{2,1,0:T(8,128)(2,1)S(1)}, bf16[128,6,64]{2,1,0:T...) while((s32[]{:T(128)}, f32[49,6,128]{2,1,0:T(8,128)S(1)}, ...), condition=%wide.region_1.0_spmd, body=%wide.region_0.0_spmd.sunk | while | flops 197396 | bytes 608564 | solution.py:120
  184.7 4.1 exp.21
  188.7 68.9 %while.68 = (s32[]{:T(128)}, f32[128,6,64]{2,1,0:T(8,128)S(1)}, f32[49,6,128]{1,2,0:T(8,128)}, bf16[14,22,768]{2,1,0:T(8,128)(2,1)S(1)}, s32[]{:T(128)}, /*index...) while((s32[]{:T(128)}, f32[128,6,64]{2,1,0:T(8,128)S(1)}, ...), condition=%wide.region_10.11_spmd.clone, body=%wide.region_9.10_spmd.clone.sunk | while | flops 196630 | bytes 1287498 | solution.py:156
  263.9 43.8 %while.66 = (s32[]{:T(128)}, f32[128,384]{0,1:T(8,128)S(1)}, f32[49,6,128]{2,1,0:T(8,128)S(1)}, bf16[14,22,768]{2,1,0:T(8,128)(2,1)S(1)}, bf16[128,6,64]{2,1,0:T...) while((s32[]{:T(128)}, f32[128,384]{0,1:T(8,128)S(1)}, ...), condition=%wide.region_13.14_spmd, body=%wide.region_12.13_spmd.sunk | while | flops 394005 | bytes 2089296 | solution.py:239
  308.8 362.1 %while.67 = (s32[]{:T(128)}, f32[14,22,768]{2,1,0:T(8,128)}, f32[49,6,128]{1,2,0:T(8,128)}, bf16[14,22,768]{2,1,0:T(8,128)(2,1)S(1)}, bf16[128,6,64]{2,1,0:T(8,1...) while((s32[]{:T(128)}, f32[14,22,768]{2,1,0:T(8,128)}, ...), condition=%wide.region_15.16_spmd, body=%wide.region_14.15_spmd.sunk | while | flops 639765 | bytes 3960160 | solution.py:258
  312.7 3.5 dynamic_update_slice.25
  320.2 3.5 dynamic_update_slice.25
  327.6 3.5 dynamic_update_slice.25
  335.0 3.5 dynamic_update_slice.25
  342.5 3.5 dynamic_update_slice.25
  349.9 3.5 dynamic_update_slice.25
  357.3 3.5 dynamic_update_slice.25
  364.8 3.5 dynamic_update_slice.25
  372.2 3.5 dynamic_update_slice.25
  379.6 3.5 dynamic_update_slice.25
  387.1 3.5 dynamic_update_slice.25
  394.5 3.5 dynamic_update_slice.25
  401.9 3.5 dynamic_update_slice.25
  409.4 3.5 dynamic_update_slice.25
  416.8 3.5 dynamic_update_slice.25
  424.2 3.5 dynamic_update_slice.25
  431.7 3.5 dynamic_update_slice.25
  439.1 3.5 dynamic_update_slice.25
  446.5 3.5 dynamic_update_slice.25
  453.9 3.5 dynamic_update_slice.25
  461.4 3.5 dynamic_update_slice.25
  468.8 3.5 dynamic_update_slice.25
  476.2 3.5 dynamic_update_slice.25
  483.7 3.5 dynamic_update_slice.25
  491.1 3.5 dynamic_update_slice.25
  498.5 3.5 dynamic_update_slice.25
  505.9 3.5 dynamic_update_slice.25
  513.4 3.5 dynamic_update_slice.25
  520.8 3.4 dynamic_update_slice.25
  528.2 3.4 dynamic_update_slice.25
  535.6 3.4 dynamic_update_slice.25
  543.0 3.4 dynamic_update_slice.25
  550.4 3.4 dynamic_update_slice.25
  557.8 3.4 dynamic_update_slice.25
  565.2 3.4 dynamic_update_slice.25
  572.6 3.4 dynamic_update_slice.25
  579.9 3.4 dynamic_update_slice.25
  587.3 3.4 dynamic_update_slice.25
  594.6 3.4 dynamic_update_slice.25
  602.0 3.4 dynamic_update_slice.25
  609.3 3.4 dynamic_update_slice.25
  616.7 3.4 dynamic_update_slice.25
  624.0 3.3 dynamic_update_slice.25
  631.3 3.3 dynamic_update_slice.25
  638.6 3.3 dynamic_update_slice.25
  645.8 3.3 dynamic_update_slice.25
  653.1 3.3 dynamic_update_slice.25
  682.7 3.5 collective-permute-start.5
  688.4 24.5 %all_gather.28 = bf16[8,16,384]{2,1,0:T(8,128)(2,1)S(1)} all-gather(bf16[1,16,384]{2,1,0:T(8,128)(2,1)S(1)} %convert_element_type.246), channel_id=1, replica_groups=mesh['gy'=4,'gx'=8] {'gx'}, dimensions={0}, use_global_device_ids=true | all-gather | bytes 110592 | tf_op jit(solution)/shard_map/all_gather | solution.py:16
  713.8 26.8 %psum.21 = bf16[16,384]{1,0:T(8,128)(2,1)S(1)} all-reduce(bf16[16,384]{1,0:T(8,128)(2,1)S(1)} %convert_element_type.238), channel_id=1, replica_groups=mesh['gy'=4,'gx'=8] {'gx'}, use_global_device_ids=true, to_apply=%region_16.17 | all-reduce | flops 6144 | bytes 24576 | tf_op jit(solution)/shard_map/psum | solution.py:212
  740.6 23.8 %all-reduce.2 = (bf16[8,384]{1,0:T(8,128)(2,1)S(1)}, bf16[8,384]{1,0:T(8,128)(2,1)S(1)}) all-reduce(bf16[8,384]{1,0:T(8,128)(2,1)S(1)} %convert_element_type.250, bf16[8,384]{1,0:T(8,128)(2,1)S(1)} %convert_element_type.242), channel_id=1, replica_groups=mesh['gy'=4,'gx'=8] {'gy'}, use_global_device_ids=true, to_apply=%region_19.20 | all-reduce | flops 6144 | bytes 24576 | tf_op jit(solution)/shard_map/psum | solution.py:217
  765.5 3.5 scatter-add.15
  (1500 shorter events, 425.8 us)
Async XLA Ops:
  0.6 1.2 copy-start
  0.6 72.9 %copy-start.2 = (bf16[384,384]{1,0:T(8,128)(2,1)S(1)}, bf16[384,384]{1,0:T(8,128)(2,1)}, u32[]{:S(2)}) copy-start(bf16[384,384]{1,0:T(8,128)(2,1)} %param.23) | copy-start | bytes 884740
  3.1 71.6 %collective-permute-start = (bf16[3,16,768]{2,1,0:T(8,128)(2,1)S(1)}, bf16[3,16,768]{2,1,0:T(8,128)(2,1)S(1)}, u32[]{:S(2)}, u32[]{:S(2)}) collective-permute-start(bf16[3,16,768]{2,1,0:T(8,128)(2,1)S(1)} %get-tuple-element.770), channel_id=1, source_target_pairs={{0,8},{8,16},{16,24},{1,9},{9,17},{17,25},{2,10},{10,18},{18,26},{... | collective-permute-start | bytes 221192 | tf_op jit(solution)/shard_map/ppermute | solution.py:30
  7.6 67.1 %collective-permute-start.1 = (bf16[3,16,768]{2,1,0:T(8,128)(2,1)S(1)}, bf16[3,16,768]{2,1,0:T(8,128)(2,1)S(1)}, u32[]{:S(2)}, u32[]{:S(2)}) collective-permute-start(bf16[3,16,768]{2,1,0:T(8,128)(2,1)S(1)} %get-tuple-element.771), channel_id=1, source_target_pairs={{8,0},{16,8},{24,16},{9,1},{17,9},{25,17},{10,2},{18,10},{26,18},{... | collective-permute-start | bytes 221192 | tf_op jit(solution)/shard_map/ppermute | solution.py:31
  41.0 221.8 %copy-start.1 = (bf16[128,384]{0,1:T(8,128)(2,1)}, bf16[128,384]{0,1:T(8,128)(2,1)S(1)}, u32[]{:S(2)}) copy-start(bf16[128,384]{0,1:T(8,128)(2,1)S(1)} %copy.82) | copy-start | bytes 294916
  44.1 34.2 %copy-start.5 = (bf16[16,6,64]{2,1,0:T(8,128)(2,1)}, bf16[16,6,64]{2,1,0:T(8,128)(2,1)S(1)}, u32[]{:S(2)}) copy-start(bf16[16,6,64]{2,1,0:T(8,128)(2,1)S(1)} %reshape.422) | copy-start | bytes 36868
  62.5 11.0 %copy-start.8 = (bf16[8,6,64]{2,1,0:T(8,128)(2,1)}, bf16[8,6,64]{2,1,0:T(8,128)(2,1)S(1)}, u32[]{:S(2)}) copy-start(bf16[8,6,64]{2,1,0:T(8,128)(2,1)S(1)} %reshape.423) | copy-start | bytes 18436
  74.8 36.3 %collective-permute-start.2 = (bf16[14,3,768]{2,1,0:T(4,128)(2,1)S(1)}, bf16[14,3,768]{2,1,0:T(4,128)(2,1)S(1)}, u32[]{:S(2)}, u32[]{:S(2)}) collective-permute-start(bf16[14,3,768]{2,1,0:T(4,128)(2,1)S(1)} %get-tuple-element.765), channel_id=1, source_target_pairs={{0,1},{1,2},{2,3},{3,4},{4,5},{5,6},{6,7},{8,9},{9,10},{10,11},{11... | collective-permute-start | bytes 193544 | tf_op jit(solution)/shard_map/ppermute | solution.py:30
  76.1 35.0 %collective-permute-start.3 = (bf16[14,3,768]{2,1,0:T(4,128)(2,1)S(1)}, bf16[14,3,768]{2,1,0:T(4,128)(2,1)}, u32[]{:S(2)}, u32[]{:S(2)}) collective-permute-start(bf16[14,3,768]{2,1,0:T(4,128)(2,1)S(1)} %get-tuple-element.766), channel_id=1, source_target_pairs={{1,0},{2,1},{3,2},{4,3},{5,4},{6,5},{7,6},{9,8},{10,9},{11,10},{12... | collective-permute-start | bytes 193544 | tf_op jit(solution)/shard_map/ppermute | solution.py:31
  112.2 69.8 %copy-start.11 = (f32[6,128]{1,0:T(8,128)S(1)}, f32[6,128]{1,0:T(8,128)}, u32[]{:S(2)}) copy-start(f32[6,128]{1,0:T(8,128)} %get-tuple-element.776) | copy-start | bytes 9220
  112.2 69.8 %copy-start.12 = (f32[6,128]{1,0:T(8,128)S(1)}, f32[6,128]{1,0:T(8,128)}, u32[]{:S(2)}) copy-start(f32[6,128]{1,0:T(8,128)} %get-tuple-element.774) | copy-start | bytes 9220
  182.2 79.6 %copy-start.3 = (f32[6,128]{1,0:T(8,128)}, f32[6,128]{1,0:T(8,128)S(1)}, u32[]{:S(2)}) copy-start(f32[6,128]{1,0:T(8,128)S(1)} %log_add_fusion) | copy-start | bytes 9220
  188.7 69.1 %copy-start.4 = (bf16[16,6,64]{2,1,0:T(8,128)(2,1)S(1)}, bf16[16,6,64]{2,1,0:T(8,128)(2,1)}, u32[]{:S(2)}) copy-start(bf16[16,6,64]{2,1,0:T(8,128)(2,1)} %reshape.424) | copy-start | bytes 36868
  257.6 5.0 copy-start.6
  257.6 6.1 copy-start.9
  259.2 4.7 copy-start.7
  671.9 5.8 collective-permute-start.4
  676.8 103.7 %copy-start.10 = (bf16[8,16,384]{2,1,0:T(8,128)(2,1)S(1)}, bf16[8,16,384]{2,1,0:T(8,128)(2,1)}, u32[]{:S(2)}) copy-start(bf16[8,16,384]{2,1,0:T(8,128)(2,1)} %param.25) | copy-start | bytes 294916
  682.7 81.7 %collective-permute-start.5 = (bf16[14,3,768]{2,1,0:T(4,128)(2,1)S(1)}, bf16[14,3,768]{2,1,0:T(4,128)(2,1)S(1)}, u32[]{:S(2)}, u32[]{:S(2)}) collective-permute-start(bf16[14,3,768]{2,1,0:T(4,128)(2,1)S(1)} %slice.249), channel_id=1, source_target_pairs={{0,1},{1,2},{2,3},{3,4},{4,5},{5,6},{6,7},{8,9},{9,10},{10,11},{11... | collective-permute-start | bytes 193544 | tf_op jit(solution)/shard_map/ppermute | solution.py:39
  769.9 6.2 collective-permute-start.6
  777.1 3.3 collective-permute-start.7
